TPU v7x, 32 devices: a whole 2x2x4 slice. The times are simulated.
32 devices in a mesh: seq: 8 (over y, x, core), head: 4 (over z).
Axes of the slice: x: 2, y: 2, z: 4, core: 2. Of those that a mesh axis runs over, the one named last changes fastest.
Arguments:
- qk: bfloat16 [16384, 2048], P('seq', 'head'), may hold values from -480 to 480, as said below
- values: bfloat16 [16384, 2048], P('seq', 'head'), may hold values from -6 to 6
- bucket: int32 [64, 16], replicated, may hold values from 0 to 1
- pair_row: int32 [8, 8, 3], P('seq'), may hold values from 0 to 7, as said below
- pair_col: int32 [8, 8, 3], P('seq'), may hold values from 0 to 7, as said below
- pair_count: int32 [8, 8], P('seq'), may hold values from 0 to 3, as said below
- w_out: bfloat16 [2048, 2048], P('head'), may hold values from -0.125 to 0.125
Outputs:
- projected: bfloat16 [16384, 2048], P(('seq', 'head'))
Inputs may be any that keep to these rules, and one draw needn't show every extreme that they name: `pair_row`: every value is a local block index of the shard it refers to. `pair_col`: every value is a local block index; a pair never joins a block with itself. `pair_count`: some shard has 3 live slots towards every shard in every draw. `qk`: row scales of the vectors may differ widely.
All inputs are finite; a program needn't handle non-finite values.
Results may differ from a plain program's by a relative error of at most 0.014.
Values may be sent and summed in bfloat16 or wider, within the bound.
No kernel may reach another device: no remote copies, remote signals or barrier semaphores. Data moves between devices by JAX's collectives and lax.ppermute only.
A program may use at most 128 MiB of HBM per device.

v0:
```python
import math
import jax
import jax.numpy as jnp
from jax import lax
from jax.sharding import PartitionSpec as P

HD = 128
BLOCK = 256
NEG = -1e30


def inverse_norms(block):
    wide = block.astype(jnp.float32)
    return (lax.rsqrt(jnp.mean(wide * wide, axis=-1) + 1e-06) / math.sqrt(block.shape[-1])).T


def softmax_side(scores, axis):
    top = jnp.max(scores, axis=axis)
    weights = jnp.exp(scores - jnp.expand_dims(top, axis))
    total = jnp.sum(weights, axis=axis)
    return (top, total, weights.astype(jnp.bfloat16))


def pair_parts(q_a, v_a, q_b, v_b, keep):
    gram = jnp.einsum("shd,thd->hst", q_a, q_b, preferred_element_type=jnp.float32)
    srow = gram * inverse_norms(q_b)[:, None, :]
    scol = gram * inverse_norms(q_a)[:, :, None]
    mrow, lrow, prow = softmax_side(srow, 2)
    acc_row = jnp.einsum("hst,thd->shd", prow, v_b, preferred_element_type=jnp.float32)
    mcol, lcol, pcol = softmax_side(scol, 1)
    acc_col = jnp.einsum("hst,shd->thd", pcol, v_a, preferred_element_type=jnp.float32)
    mrow = jnp.where(keep[:, None], mrow, NEG)
    lrow = jnp.where(keep[:, None], lrow, 0.0)
    acc_row = jnp.where(keep[None, :, None], acc_row, 0.0)
    mcol = jnp.where(keep[:, None], mcol, NEG)
    lcol = jnp.where(keep[:, None], lcol, 0.0)
    acc_col = jnp.where(keep[None, :, None], acc_col, 0.0)
    return ((mrow, lrow, acc_row), (mcol, lcol, acc_col))


def diagonal_parts(q_a, v_a):
    gram = jnp.einsum("shd,thd->hst", q_a, q_a, preferred_element_type=jnp.float32)
    srow = gram * inverse_norms(q_a)[:, None, :]
    eye = jnp.arange(q_a.shape[0])[:, None] == jnp.arange(q_a.shape[0])[None, :]
    srow = jnp.where(eye[None], NEG, srow)
    mrow, lrow, prow = softmax_side(srow, 2)
    acc_row = jnp.einsum("hst,thd->shd", prow, v_a, preferred_element_type=jnp.float32)
    return (mrow, lrow, acc_row)


def group_parts(item):
    q_a, v_a, q_b, v_b, keep = item
    return jax.vmap(pair_parts)(q_a, v_a, q_b, v_b, keep)


def body(qk, values, bucket, pair_row, pair_col, pair_count, w_out):
    shards = lax.axis_size("seq")
    seq_dev, width = qk.shape
    heads_here = width // HD
    blocks_here = seq_dev // BLOCK
    slots = pair_row.shape[2]
    total_slots = shards * slots
    q_blocks = qk.reshape(blocks_here, BLOCK, heads_here, HD)
    v_blocks = values.reshape(blocks_here, BLOCK, heads_here, HD)
    wanted = lax.all_to_all(pair_col, "seq", split_axis=1, concat_axis=0, tiled=True).reshape(
        total_slots
    )
    sent_q = q_blocks[wanted].reshape(shards, slots, BLOCK, heads_here, HD)
    sent_v = v_blocks[wanted].reshape(shards, slots, BLOCK, heads_here, HD)
    got_q, got_v = (
        lax.all_to_all(sent_q, "seq", split_axis=0, concat_axis=0, tiled=True),
        lax.all_to_all(sent_v, "seq", split_axis=0, concat_axis=0, tiled=True),
    )
    row_index = pair_row.reshape(total_slots)
    seq_id = lax.axis_index("seq")
    head_id = lax.axis_index("head")
    my_buckets = lax.dynamic_slice_in_dim(bucket, head_id * heads_here, heads_here, 1)
    row_glob = seq_id * blocks_here + row_index
    owner = jnp.repeat(jnp.arange(shards, dtype=jnp.int32), slots)
    col_glob = owner * blocks_here + pair_col.reshape(total_slots)
    live = (jnp.arange(slots, dtype=jnp.int32)[None, :] < pair_count[0][:, None]).reshape(
        total_slots
    )
    keep = live[:, None] & (my_buckets[row_glob] == my_buckets[col_glob])
    mine_q = q_blocks[row_index].reshape(shards, slots, BLOCK, heads_here, HD)
    mine_v = v_blocks[row_index].reshape(shards, slots, BLOCK, heads_here, HD)
    row_side, col_side = lax.map(
        group_parts, (mine_q, mine_v, got_q, got_v, keep.reshape(shards, slots, heads_here))
    )
    back_m, back_l, back_acc = lax.all_to_all(
        col_side, "seq", split_axis=0, concat_axis=0, tiled=True
    )
    diag_m, diag_l, diag_acc = jax.vmap(diagonal_parts)(q_blocks, v_blocks)
    index_all = jnp.concatenate([row_index, wanted], axis=0)
    m_all = jnp.concatenate(
        [
            row_side[0].reshape(total_slots, heads_here, BLOCK),
            back_m.reshape(total_slots, heads_here, BLOCK),
        ],
        axis=0,
    )
    l_all = jnp.concatenate(
        [
            row_side[1].reshape(total_slots, heads_here, BLOCK),
            back_l.reshape(total_slots, heads_here, BLOCK),
        ],
        axis=0,
    )
    acc_all = jnp.concatenate(
        [
            row_side[2].reshape(total_slots, BLOCK, heads_here, HD),
            back_acc.reshape(total_slots, BLOCK, heads_here, HD),
        ],
        axis=0,
    )
    onehot = index_all[:, None] == jnp.arange(blocks_here, dtype=jnp.int32)[None, :]
    m_tot = jnp.maximum(
        diag_m, jnp.max(jnp.where(onehot[:, :, None, None], m_all[:, None], NEG), axis=0)
    )
    m_at = jnp.sum(jnp.where(onehot[:, :, None, None], m_tot[None], 0.0), axis=1)
    scale_all = jnp.exp(m_all - m_at)
    onehot_f = onehot.astype(jnp.float32)
    scale_diag = jnp.exp(diag_m - m_tot)
    l_tot = diag_l * scale_diag + jnp.einsum(
        "kb,khs->bhs", onehot_f, l_all * scale_all, precision=lax.Precision.HIGHEST
    )
    weighted = acc_all * jnp.transpose(scale_all, (0, 2, 1))[..., None]
    acc_tot = diag_acc * jnp.transpose(scale_diag, (0, 2, 1))[..., None]
    acc_tot = acc_tot + jnp.einsum(
        "kb,kshd->bshd", onehot_f, weighted, precision=lax.Precision.HIGHEST
    )
    attn = (
        (acc_tot / jnp.transpose(l_tot, (0, 2, 1))[..., None])
        .reshape(seq_dev, width)
        .astype(jnp.bfloat16)
    )
    mixed = lax.all_to_all(attn, "head", split_axis=0, concat_axis=1, tiled=True)
    summed = jnp.dot(
        mixed, lax.all_gather(w_out, "head", axis=0, tiled=True), preferred_element_type=jnp.float32
    )
    return summed.astype(jnp.bfloat16)


def solution(mesh):
    return jax.shard_map(
        body,
        mesh=mesh,
        in_specs=(
            P("seq", "head"),
            P("seq", "head"),
            P(),
            P("seq", None, None),
            P("seq", None, None),
            P("seq", None),
            P("head", None),
        ),
        out_specs=P(("seq", "head"), None),
        check_vma=False,
    )
```

profile of v0, /device:TPU:2, one launch (start us, length us, event | category | flops | bytes accessed | tf_op | source)
XLA Modules:
  0.0 551.1 jit_solution(3559827569345628649)
XLA Ops:
  7.9 4.3 all-to-all-start
  12.2 4.0 reshape.322
  16.1 2.1 copy.208
  18.3 4.4 gather_fusion.3
  22.7 4.7 all-to-all-start.1
  27.4 4.0 reshape.323
  31.4 3.4 copy.213
  34.8 5.9 %gather_fusion.4 = bf16[24,256,4,128]{3,1,2,0:T(8,128)(2,1)} fusion(bf16[8,256,4,128]{3,1,2,0:T(8,128)(2,1)} %copy.213, s32[1024]{0:T(1024)S(1)} %pad_clamp_fusion), kind=kCustom, calls=%fused_computation.4 | custom fusion | bytes 12583008 | tf_op jit(solution)/shard_map/gather | solution.py:69
  40.7 8.6 %copy.225 = bf16[8,3,256,4,128]{2,4,3,1,0:T(8,128)(2,1)} copy(bf16[8,3,256,4,128]{4,2,3,1,0:T(8,128)(2,1)} %bitcast.132) | data formatting | bytes 12582912 | tf_op jit(solution)/shard_map/reshape | solution.py:69
  49.3 48.2 %all-to-all-done.1 = bf16[8,3,256,4,128]{4,2,3,1,0:T(8,128)(2,1)} async-done(((bf16[8,3,256,4,128]{4,2,3,1,0:T(8,128)(2,1)}), bf16[8,3,256,4,128]{4,2,3,1,0:T(8,128)(2,1)}, u32[]{:S(2)}, u32[]{:S(2)}) %all-to-all-start.1) | async-done | bytes 6291488 | tf_op jit(solution)/shard_map/all_to_all | solution.py:71
  97.6 6.2 %all-to-all-start.2 = ((bf16[8,3,256,4,128]{2,4,3,1,0:T(8,128)(2,1)}), bf16[8,3,256,4,128]{2,4,3,1,0:T(8,128)(2,1)}, u32[]{:S(2)}, u32[]{:S(2)}) async-start(bf16[8,3,256,4,128]{2,4,3,1,0:T(8,128)(2,1)} %copy.225), calls=%async_computation.2 | async-start | bytes 12582912 | tf_op jit(solution)/shard_map/all_to_all | solution.py:72
  104.0 4.4 gather_fusion.2
  108.5 5.9 %gather_fusion.5 = bf16[24,256,4,128]{3,1,2,0:T(8,128)(2,1)} fusion(bf16[8,256,4,128]{3,1,2,0:T(8,128)(2,1)} %copy.213, s32[1024]{0:T(1024)S(1)} %get-tuple-element.203), kind=kCustom, calls=%fused_computation.5 | custom fusion | bytes 12583008 | tf_op jit(solution)/shard_map/gather | solution.py:86
  116.3 57.7 %all-to-all-done.2 = bf16[8,3,256,4,128]{2,4,3,1,0:T(8,128)(2,1)} async-done(((bf16[8,3,256,4,128]{2,4,3,1,0:T(8,128)(2,1)}), bf16[8,3,256,4,128]{2,4,3,1,0:T(8,128)(2,1)}, u32[]{:S(2)}, u32[]{:S(2)}) %all-to-all-start.2) | async-done | bytes 6291488 | tf_op jit(solution)/shard_map/all_to_all | solution.py:72
  173.9 103.8 %while.20 = (s32[]{:T(128)}, f32[8,3,4,256]{3,2,1,0:T(4,128)S(1)}, f32[8,3,4,256]{3,2,1,0:T(4,128)S(1)}, f32[8,3,256,4,128]{2,4,3,1,0:T(8,128)}, f32[8,3,4,256]{...) while((s32[]{:T(128)}, f32[8,3,4,256]{3,2,1,0:T(4,128)S(1)}, ...), condition=%wide.region_9.10_spmd, body=%wide.region_2.9_spmd.sunk | while | flops 619720704 | bytes 20795064 | solution.py:87
  173.9 2.3 multiply_reduce_fusion.7
  176.3 2.5 multiply_reduce_fusion.8
  178.8 3.3 bitcast_dynamic-update-slice_fusion.5
  182.0 3.2 bitcast_dynamic-update-slice_fusion.4
  187.0 2.3 multiply_reduce_fusion.7
  189.3 2.5 multiply_reduce_fusion.8
  191.8 3.2 bitcast_dynamic-update-slice_fusion.5
  195.0 3.1 bitcast_dynamic-update-slice_fusion.4
  199.9 2.3 multiply_reduce_fusion.7
  202.3 2.5 multiply_reduce_fusion.8
  204.8 3.2 bitcast_dynamic-update-slice_fusion.5
  208.0 3.1 bitcast_dynamic-update-slice_fusion.4
  212.9 2.3 multiply_reduce_fusion.7
  215.2 2.5 multiply_reduce_fusion.8
  217.7 3.2 bitcast_dynamic-update-slice_fusion.5
  220.9 3.2 bitcast_dynamic-update-slice_fusion.4
  225.9 2.3 multiply_reduce_fusion.7
  228.2 2.5 multiply_reduce_fusion.8
  230.7 3.2 bitcast_dynamic-update-slice_fusion.5
  233.9 3.1 bitcast_dynamic-update-slice_fusion.4
  238.9 2.3 multiply_reduce_fusion.7
  241.2 2.5 multiply_reduce_fusion.8
  243.7 3.2 bitcast_dynamic-update-slice_fusion.5
  246.9 3.1 bitcast_dynamic-update-slice_fusion.4
  251.9 2.3 multiply_reduce_fusion.7
  254.2 2.5 multiply_reduce_fusion.8
  256.7 3.2 bitcast_dynamic-update-slice_fusion.5
  259.8 3.2 bitcast_dynamic-update-slice_fusion.4
  264.8 2.3 multiply_reduce_fusion.7
  267.1 2.5 multiply_reduce_fusion.8
  269.7 3.2 bitcast_dynamic-update-slice_fusion.5
  272.9 3.1 bitcast_dynamic-update-slice_fusion.4
  277.8 7.6 %all_to_all.50 = f32[8,3,4,256]{3,2,1,0:T(4,128)S(1)} all-to-all(f32[8,3,4,256]{3,2,1,0:T(4,128)S(1)} %get-tuple-element.73), channel_id=1, replica_groups=mesh['seq'=8,'head'=4] {'seq'}, dimensions={0} | all-to-all | bytes 196608 | tf_op jit(solution)/shard_map/all_to_all | solution.py:90
  285.4 7.6 %all_to_all.51 = f32[8,3,4,256]{3,2,1,0:T(4,128)S(1)} all-to-all(f32[8,3,4,256]{3,2,1,0:T(4,128)S(1)} %get-tuple-element.77), channel_id=1, replica_groups=mesh['seq'=8,'head'=4] {'seq'}, dimensions={0} | all-to-all | bytes 196608 | tf_op jit(solution)/shard_map/all_to_all | solution.py:90
  293.0 6.8 %all-to-all-start.4 = ((f32[8,3,256,4,128]{2,4,3,1,0:T(8,128)}), f32[8,3,256,4,128]{2,4,3,1,0:T(8,128)}, u32[]{:S(2)}, u32[]{:S(2)}) async-start(f32[8,3,256,4,128]{2,4,3,1,0:T(8,128)} %get-tuple-element.75), calls=%async_computation.4 | async-start | bytes 25165824 | tf_op jit(solution)/shard_map/all_to_all | solution.py:90
  300.6 2.4 copy.242
  303.1 2.0 multiply_reduce_fusion.4
  305.2 1.7 fusion.37
  306.9 3.2 copy-done.3
  310.1 2.9 fusion.38
  314.4 13.2 %copy.230 = f32[24,256,4,128]{3,0,2,1:T(8,128)} copy(f32[24,256,4,128]{1,3,2,0:T(8,128)} %bitcast.134) | data formatting | bytes 25165824 | tf_op jit(solution)/shard_map/reshape | solution.py:111
  329.1 108.3 %all-to-all-done.4 = f32[8,3,256,4,128]{2,4,3,1,0:T(8,128)} async-done(((f32[8,3,256,4,128]{2,4,3,1,0:T(8,128)}), f32[8,3,256,4,128]{2,4,3,1,0:T(8,128)}, u32[]{:S(2)}, u32[]{:S(2)}) %all-to-all-start.4) | async-done | bytes 12582944 | tf_op jit(solution)/shard_map/all_to_all | solution.py:90
  437.4 12.9 %copy.231 = f32[24,256,4,128]{3,0,2,1:T(8,128)} copy(f32[24,256,4,128]{1,3,2,0:T(8,128)} %bitcast.33) | data formatting | bytes 25165824 | tf_op jit(solution)/shard_map/reshape | solution.py:112
  450.3 15.0 %fusion.33 = f32[8,256,4,128]{3,0,2,1:T(8,128)S(1)} fusion(f32[24,256,4,128]{3,0,2,1:T(8,128)} %copy.231, f32[24,256,4,128]{3,0,2,1:T(8,128)} %copy.230, f32[48,256,4]{0,2,1:T(4,128)S(1)} %copy.233, s32[48]{0:T(128)S(1)} %pad_add_fusion), kind=kOutput, calls=%fused_computation.49 | convolution fusion | flops 616563072 | bytes 29556928 | tf_op jit(solution)/shard_map/kb,kshd->bshd/dot_general | solution.py:129
  465.4 9.4 %fusion.44 = bf16[8,256,4,128]{3,1,2,0:T(8,128)(2,1)S(1)} fusion(f32[8,256,4,128]{3,0,2,1:T(8,128)S(1)} %fusion.33, f32[8,256,4]{1,2,0:T(4,128)S(1)} %copy.237, f32[8,256,4]{1,2,0:T(4,128)S(1)} %copy.229, f32[8,4,256,256]{2,3,1,0:T(8,128)} %copy-done.3, f32[8,4,256]{2,1,0:T(4,128)S(1)} %get-tuple-element.201, f32[8,4,256]{2,1,0:T(4,128)S(1)} %copy.210, ...), kind=kOutput, calls=%fused_computation.62 | convolution fusion | flops 549453824 | bytes 16973824 | tf_op jit(solution)/shard_map/vmap(hst,thd->shd)/dot_general | solution.py:47
  476.4 2.2 convert_element_type.32
  478.6 53.3 %all_to_all.52 = bf16[4,512,512]{2,1,0:T(8,128)(2,1)S(1)} all-to-all(bf16[4,512,512]{2,1,0:T(8,128)(2,1)} %convert_element_type.32), channel_id=1, replica_groups=mesh['seq'=8,'head'=4] {'head'}, dimensions={0} | all-to-all | bytes 4194304 | tf_op jit(solution)/shard_map/all_to_all | solution.py:137
  531.9 2.4 copy.239
  534.3 9.9 %convolution_convert_fusion = bf16[512,2048]{1,0:T(8,128)(2,1)} fusion(bf16[512,2048]{0,1:T(8,128)(2,1)} %bitcast.136, bf16[2048,2048]{1,0:T(8,128)(2,1)} %all-gather.2.cloned.1.call-done), kind=kOutput, calls=%fused_computation.68 | convolution fusion | flops 4296015872 | bytes 12582912 | tf_op jit(solution)/shard_map/dot_general | solution.py:138
  (110 shorter events, 23.6 us)
Async XLA Ops:
  6.5 107.9 %copy-start = (s32[64,16]{0,1:T(8,128)S(1)}, s32[64,16]{0,1:T(8,128)}, u32[]{:S(2)}) copy-start(s32[64,16]{0,1:T(8,128)} %param.11) | copy-start | bytes 12292
  7.9 10.3 %all-to-all-start = ((s32[1,8,3]{2,0,1:T(1,128)}), s32[1,8,3]{2,0,1:T(1,128)S(1)}, u32[]{:S(2)}, u32[]{:S(2)}) async-start(s32[1,8,3]{2,0,1:T(1,128)} %copy.216), calls=%async_computation | async-start | bytes 8192 | tf_op jit(solution)/shard_map/all_to_all | solution.py:65
  22.7 74.9 %all-to-all-start.1 = ((bf16[8,3,256,4,128]{4,2,3,1,0:T(8,128)(2,1)}), bf16[8,3,256,4,128]{4,2,3,1,0:T(8,128)(2,1)}, u32[]{:S(2)}, u32[]{:S(2)}) async-start(bf16[8,3,256,4,128]{4,2,3,1,0:T(8,128)(2,1)} %bitcast.131), calls=%async_computation.1 | async-start | bytes 12582912 | tf_op jit(solution)/shard_map/all_to_all | solution.py:71
  49.3 54.5 %copy-start.5 = (s32[1,8,3]{1,0,2:T(1,128)S(1)}, s32[1,8,3]{1,0,2:T(1,128)}, u32[]{:S(2)}) copy-start(s32[1,8,3]{1,0,2:T(1,128)} %param.13) | copy-start | bytes 292
  49.3 54.5 %copy-start.6 = (s32[1,8,3]{1,0,2:T(1,128)S(1)}, s32[1,8,3]{1,0,2:T(1,128)}, u32[]{:S(2)}) copy-start(s32[1,8,3]{1,0,2:T(1,128)} %param.12) | copy-start | bytes 292
  97.6 76.4 %all-to-all-start.2 = ((bf16[8,3,256,4,128]{2,4,3,1,0:T(8,128)(2,1)}), bf16[8,3,256,4,128]{2,4,3,1,0:T(8,128)(2,1)}, u32[]{:S(2)}, u32[]{:S(2)}) async-start(bf16[8,3,256,4,128]{2,4,3,1,0:T(8,128)(2,1)} %copy.225), calls=%async_computation.2 | async-start | bytes 12582912 | tf_op jit(solution)/shard_map/all_to_all | solution.py:72
  108.5 7.6 %copy-start.7 = (s32[1,8]{1,0:T(1,128)S(1)}, s32[1,8]{1,0:T(1,128)}, u32[]{:S(2)}) copy-start(s32[1,8]{1,0:T(1,128)} %param.14) | copy-start | bytes 100
  293.0 7.6 %copy-start.2 = (bf16[8,256,4,128]{3,2,1,0:T(4,128)(2,1)S(1)}, bf16[8,256,4,128]{3,2,1,0:T(4,128)(2,1)}, u32[]{:S(2)}) copy-start(bf16[8,256,4,128]{3,2,1,0:T(4,128)(2,1)} %reshape.322) | copy-start | bytes 6291460
  293.0 144.4 %all-to-all-start.4 = ((f32[8,3,256,4,128]{2,4,3,1,0:T(8,128)}), f32[8,3,256,4,128]{2,4,3,1,0:T(8,128)}, u32[]{:S(2)}, u32[]{:S(2)}) async-start(f32[8,3,256,4,128]{2,4,3,1,0:T(8,128)} %get-tuple-element.75), calls=%async_computation.4 | async-start | bytes 25165824 | tf_op jit(solution)/shard_map/all_to_all | solution.py:90
  299.8 234.5 %all-gather.2.cloned.1.call-start = ((), (), s32[]{:S(2)}) async-start(), calls=%async_computation.7 | async-start | bytes 10485760 | tf_op jit(solution)/shard_map/all_gather | solution.py:139
  306.9 3.2 copy-start.3
  450.3 15.0 %copy-start.4 = (bf16[8,256,4,128]{3,2,1,0:T(4,128)(2,1)S(1)}, bf16[8,256,4,128]{3,2,1,0:T(4,128)(2,1)}, u32[]{:S(2)}) copy-start(bf16[8,256,4,128]{3,2,1,0:T(4,128)(2,1)} %reshape.323) | copy-start | bytes 6291460
  534.3 9.9 %copy-start.1 = (s32[64,16]{0,1:T(8,128)S(1)}, s32[64,16]{0,1:T(8,128)}, u32[]{:S(2)}) copy-start(s32[64,16]{0,1:T(8,128)} %param.11) | copy-start | bytes 12292
Sparse Core Ops, SparseCore 0:
  302.2 150.7 all-gather.1
where the time goes:
time: 553 us; the launch traced here: 551 us
  waiting for transfers between devices  215 us (39%)
  matrix products  107 us (19%)
  local copies, waits for them, and re-layouts  85.2 us (15%)
  blocking collectives  68.5 us (12%)
  other arithmetic  39.5 us (7%)
  starting transfers between devices  22 us (4%)
  between operations  13.6 us (2%)
    all_to_all x1, waiting for transfers between devices, body(): lax.all_to_all(col_side, 'seq', split_axis=0, concat_axis=0, tiled=True)  108 us
    all_to_all x1, waiting for transfers between devices, body(): lax.all_to_all(sent_v, 'seq', split_axis=0, concat_axis=0, tiled=True)  57.7 us
    all_to_all x1, blocking collectives, body(): lax.all_to_all(attn, 'head', split_axis=0, concat_axis=1, tiled=True)  53.3 us
    all_to_all x1, waiting for transfers between devices, body(): lax.all_to_all(sent_q, 'seq', split_axis=0, concat_axis=0, tiled=True)  48.2 us
    dot_general x8, matrix products, pair_parts(): jnp.einsum('hst,shd->thd', pcol, v_a, preferred_element_type=jnp.float32)  25.6 us
    dot_general x8, matrix products, pair_parts(): jnp.einsum('hst,thd->shd', prow, v_b, preferred_element_type=jnp.float32)  25.1 us
    reduce_sum x9, other arithmetic, inverse_norms(): jnp.mean(wide * wide, axis=-1) + 1e-06  20.1 us
    dot_general x8, matrix products, pair_parts(): jnp.einsum('shd,thd->hst', q_a, q_b, preferred_element_type=jnp.float32)  19.9 us
  transfers between devices with their start and end apart: 5, of which 3 were waited for; matrix products, arithmetic and copies ran while one was open for 20% of the time, Pallas kernels for 0%

commit v1 on v0

--- a/solution.py
+++ b/solution.py
@@ -7,6 +7,28 @@
 HD = 128
 BLOCK = 256
 NEG = -1e30
+
+
+def in_blocks(shard, dim, size):
+    before, after = (shard.shape[:dim], shard.shape[dim + 1 :])
+    return jnp.moveaxis(shard.reshape(*before, size, -1, *after), dim, 0)
+
+
+def in_order(parts, dim):
+    parts = jnp.moveaxis(parts, 0, dim)
+    dims = parts.shape
+    return parts.reshape(*dims[:dim], dims[dim] * dims[dim + 1], *dims[dim + 2 :])
+
+
+def rotated_exchange(x, axis, split_dim, concat_dim):
+    size, here = (lax.axis_size(axis), lax.axis_index(axis))
+    blocks = in_blocks(x, split_dim, size)
+    gathered = [blocks[here]]
+    for step in range(1, size):
+        sent = blocks[(here + step) % size]
+        gathered.append(lax.ppermute(sent, axis, [(i, (i + step) % size) for i in range(size)]))
+    blocks = jnp.stack(gathered)[(here - jnp.arange(size)) % size]
+    return in_order(blocks, concat_dim)
 
 
 def inverse_norms(block):
@@ -68,7 +90,7 @@
     sent_q = q_blocks[wanted].reshape(shards, slots, BLOCK, heads_here, HD)
     sent_v = v_blocks[wanted].reshape(shards, slots, BLOCK, heads_here, HD)
     got_q, got_v = (
-        lax.all_to_all(sent_q, "seq", split_axis=0, concat_axis=0, tiled=True),
+        rotated_exchange(sent_q, "seq", 0, 0),
         lax.all_to_all(sent_v, "seq", split_axis=0, concat_axis=0, tiled=True),
     )
     row_index = pair_row.reshape(total_slots)

time: 553 us -> 562 us (1.016)
  waiting for transfers between devices: 215 us -> 184 us
  local copies, waits for them, and re-layouts: 85.2 us -> 108 us
  starting transfers between devices: 22 us -> 37.1 us
    ppermute x0 -> x7, waiting for transfers between devices: none -> 74.7 us  [rotated_exchange(): lax.ppermute(sent, axis, [(i, (i + step) % size) for i in range(size)])]
    all_to_all x1, waiting for transfers between devices: 57.7 us -> 0.01 us  [body(): lax.all_to_all(sent_v, 'seq', split_axis=0, concat_axis=0, tiled=True)]
    all_to_all x1 -> x0, waiting for transfers between devices: 48.2 us -> none  [body(): lax.all_to_all(sent_q, 'seq', split_axis=0, concat_axis=0, tiled=True)]
    ppermute x0 -> x7, starting transfers between devices: none -> 21 us  [rotated_exchange(): lax.ppermute(sent, axis, [(i, (i + step) % size) for i in range(size)])]
    unnamed x20 -> x24, local copies, waits for them, and re-layouts: 4.83 us -> 14.6 us
    gather x0 -> x1, local copies, waits for them, and re-layouts: none -> 6.72 us  [rotated_exchange(): blocks = jnp.stack(gathered)[(here - jnp.arange(size)) % size]]
  transfers between devices with their start and end apart: 5 -> 11, of which waited for: 3 -> 5; matrix products, arithmetic and copies ran while one was open for 20% -> 22% of each run, Pallas kernels for 0% -> 0%
where the time goes in v1:
time: 562 us; the launch traced here: 560 us
  waiting for transfers between devices  184 us (33%)
  local copies, waits for them, and re-layouts  108 us (19%)
  matrix products  107 us (19%)
  blocking collectives  70.4 us (13%)
  other arithmetic  39.5 us (7%)
  starting transfers between devices  37.1 us (7%)
  between operations  13.7 us (2%)
    all_to_all x1, waiting for transfers between devices, body(): lax.all_to_all(col_side, 'seq', split_axis=0, concat_axis=0, tiled=True)  108 us
    ppermute x7, waiting for transfers between devices, rotated_exchange(): lax.ppermute(sent, axis, [(i, (i + step) % size) for i in range(size)])  74.7 us
    all_to_all x1, blocking collectives, body(): lax.all_to_all(attn, 'head', split_axis=0, concat_axis=1, tiled=True)  53.3 us
    dot_general x8, matrix products, pair_parts(): jnp.einsum('hst,shd->thd', pcol, v_a, preferred_element_type=jnp.float32)  25.6 us
    dot_general x8, matrix products, pair_parts(): jnp.einsum('hst,thd->shd', prow, v_b, preferred_element_type=jnp.float32)  25.1 us
    ppermute x7, starting transfers between devices, rotated_exchange(): lax.ppermute(sent, axis, [(i, (i + step) % size) for i in range(size)])  21 us
    reduce_sum x9, other arithmetic, inverse_norms(): jnp.mean(wide * wide, axis=-1) + 1e-06  20.1 us
    dot_general x8, matrix products, pair_parts(): jnp.einsum('shd,thd->hst', q_a, q_b, preferred_element_type=jnp.float32)  19.9 us
  transfers between devices with their start and end apart: 11, of which 5 were waited for; matrix products, arithmetic and copies ran while one was open for 22% of the time, Pallas kernels for 0%

profile of v1, /device:TPU:2, one launch (start us, length us, event | category | flops | bytes accessed | tf_op | source)
XLA Modules:
  0.0 559.5 jit_solution(2798061254043671870)
XLA Ops:
  7.9 4.3 all-to-all-start
  13.1 4.0 reshape.383
  19.3 4.4 gather_fusion.5
  23.6 8.7 %copy.261 = bf16[8,3,256,4,128]{2,4,3,1,0:T(8,128)(2,1)} copy(bf16[8,3,256,4,128]{4,2,3,1,0:T(8,128)(2,1)} %bitcast.163) | data formatting | bytes 12582912 | tf_op jit(solution)/shard_map/reshape | solution.py:91
  32.3 4.8 all-to-all-start.1
  37.1 4.0 reshape.382
  41.1 3.5 copy.244
  44.7 5.9 %gather_fusion.3 = bf16[24,256,4,128]{3,1,2,0:T(8,128)(2,1)} fusion(bf16[8,256,4,128]{3,1,2,0:T(8,128)(2,1)} %copy.244, s32[1024]{0:T(1024)S(1)} %pad_clamp_fusion.1), kind=kCustom, calls=%fused_computation.3 | custom fusion | bytes 12583008 | tf_op jit(solution)/shard_map/gather | solution.py:90
  50.6 5.2 dynamic-slice_bitcast_fusion
  56.0 6.0 %gather_fusion.2 = bf16[24,256,4,128]{3,1,2,0:T(8,128)(2,1)} fusion(bf16[8,256,4,128]{3,1,2,0:T(8,128)(2,1)} %copy.244, s32[1024]{0:T(1024)S(1)} %get-tuple-element.225), kind=kCustom, calls=%fused_computation.2 | custom fusion | bytes 12583008 | tf_op jit(solution)/shard_map/gather | solution.py:107
  62.1 4.4 gather_fusion.6
  72.5 50.4 %collective-permute-done = bf16[1,3,256,4,128]{4,2,3,1,0:T(8,128)(2,1)} collective-permute-done((bf16[1,3,256,4,128]{4,2,3,1,0:T(8,128)(2,1)}, bf16[1,3,256,4,128]{4,2,3,1,0:T(8,128)(2,1)}, u32[]{:S(2)}, u32[]{:S(2)}) %collective-permute-start) | collective-permute-done | bytes 786464 | tf_op jit(solution)/shard_map/ppermute | solution.py:29
  122.8 2.3 collective-permute-start.5
  127.2 14.2 %collective-permute-start.6 = (bf16[1,3,256,4,128]{4,2,3,1,0:T(8,128)(2,1)S(1)}, bf16[1,3,256,4,128]{4,2,3,1,0:T(8,128)(2,1)S(1)}, u32[]{:S(2)}, u32[]{:S(2)}) collective-permute-start(bf16[1,3,256,4,128]{4,2,3,1,0:T(8,128)(2,1)S(1)} %get-tuple-element.209), channel_id=1, source_target_pairs={{0,28},{4,0},{8,4},{12,8},{16,12},{20,16},{24,20},{28,24},{1,29},{... | collective-permute-start | bytes 2359304 | tf_op jit(solution)/shard_map/ppermute | solution.py:29
  146.6 10.6 %collective-permute-done.4 = bf16[1,3,256,4,128]{4,2,3,1,0:T(8,128)(2,1)S(1)} collective-permute-done((bf16[1,3,256,4,128]{4,2,3,1,0:T(8,128)(2,1)}, bf16[1,3,256,4,128]{4,2,3,1,0:T(8,128)(2,1)S(1)}, u32[]{:S(2)}, u32[]{:S(2)}) %collective-permute-start.4) | collective-permute-done | bytes 786464 | tf_op jit(solution)/shard_map/ppermute | solution.py:29
  159.3 13.4 %collective-permute-done.6 = bf16[1,3,256,4,128]{4,2,3,1,0:T(8,128)(2,1)S(1)} collective-permute-done((bf16[1,3,256,4,128]{4,2,3,1,0:T(8,128)(2,1)S(1)}, bf16[1,3,256,4,128]{4,2,3,1,0:T(8,128)(2,1)S(1)}, u32[]{:S(2)}, u32[]{:S(2)}) %collective-permute-start.6) | collective-permute-done | bytes 786464 | tf_op jit(solution)/shard_map/ppermute | solution.py:29
  173.6 6.7 %gather_fusion.4 = bf16[8,3,256,4,128]{4,2,3,1,0:T(8,128)(2,1)} fusion(bf16[8,3,256,4,128]{4,2,3,1,0:T(8,128)(2,1)} %bitcast.167, s32[1024]{0:T(1024)S(1)} %pad_clamp_fusion), kind=kCustom, calls=%fused_computation.4 | custom fusion | bytes 12582944 | tf_op jit(solution)/shard_map/gather | solution.py:30
  180.3 103.7 %while.20 = (s32[]{:T(128)}, f32[8,3,4,256]{3,2,1,0:T(4,128)S(1)}, f32[8,3,4,256]{3,2,1,0:T(4,128)S(1)}, f32[8,3,256,4,128]{2,4,3,1,0:T(8,128)}, f32[8,3,4,256]{...) while((s32[]{:T(128)}, f32[8,3,4,256]{3,2,1,0:T(4,128)S(1)}, ...), condition=%wide.region_9.10_spmd, body=%wide.region_2.9_spmd.sunk | while | flops 619720704 | bytes 20795064 | solution.py:109
  180.3 2.3 multiply_reduce_fusion.7
  182.7 2.5 multiply_reduce_fusion.8
  185.2 3.2 bitcast_dynamic-update-slice_fusion.12
  188.4 3.1 bitcast_dynamic-update-slice_fusion.11
  193.3 2.3 multiply_reduce_fusion.7
  195.6 2.5 multiply_reduce_fusion.8
  198.2 3.2 bitcast_dynamic-update-slice_fusion.12
  201.3 3.1 bitcast_dynamic-update-slice_fusion.11
  206.3 2.3 multiply_reduce_fusion.7
  208.6 2.5 multiply_reduce_fusion.8
  211.1 3.2 bitcast_dynamic-update-slice_fusion.12
  214.2 3.1 bitcast_dynamic-update-slice_fusion.11
  219.2 2.3 multiply_reduce_fusion.7
  221.5 2.5 multiply_reduce_fusion.8
  224.0 3.2 bitcast_dynamic-update-slice_fusion.12
  227.2 3.1 bitcast_dynamic-update-slice_fusion.11
  232.2 2.3 multiply_reduce_fusion.7
  234.5 2.5 multiply_reduce_fusion.8
  237.0 3.2 bitcast_dynamic-update-slice_fusion.12
  240.2 3.1 bitcast_dynamic-update-slice_fusion.11
  245.1 2.3 multiply_reduce_fusion.7
  247.4 2.5 multiply_reduce_fusion.8
  249.9 3.2 bitcast_dynamic-update-slice_fusion.12
  253.1 3.2 bitcast_dynamic-update-slice_fusion.11
  258.2 2.3 multiply_reduce_fusion.7
  260.5 2.5 multiply_reduce_fusion.8
  263.0 3.2 bitcast_dynamic-update-slice_fusion.12
  266.2 3.1 bitcast_dynamic-update-slice_fusion.11
  271.2 2.3 multiply_reduce_fusion.7
  273.5 2.5 multiply_reduce_fusion.8
  276.0 3.2 bitcast_dynamic-update-slice_fusion.12
  279.2 3.1 bitcast_dynamic-update-slice_fusion.11
  284.1 9.6 %all_to_all.45 = f32[8,3,4,256]{3,2,1,0:T(4,128)S(1)} all-to-all(f32[8,3,4,256]{3,2,1,0:T(4,128)S(1)} %get-tuple-element.73), channel_id=1, replica_groups=mesh['seq'=8,'head'=4] {'seq'}, dimensions={0} | all-to-all | bytes 196608 | tf_op jit(solution)/shard_map/all_to_all | solution.py:112
  293.7 7.6 %all_to_all.46 = f32[8,3,4,256]{3,2,1,0:T(4,128)S(1)} all-to-all(f32[8,3,4,256]{3,2,1,0:T(4,128)S(1)} %get-tuple-element.77), channel_id=1, replica_groups=mesh['seq'=8,'head'=4] {'seq'}, dimensions={0} | all-to-all | bytes 196608 | tf_op jit(solution)/shard_map/all_to_all | solution.py:112
  301.2 7.1 %all-to-all-start.3 = ((f32[8,3,256,4,128]{2,4,3,1,0:T(8,128)}), f32[8,3,256,4,128]{2,4,3,1,0:T(8,128)}, u32[]{:S(2)}, u32[]{:S(2)}) async-start(f32[8,3,256,4,128]{2,4,3,1,0:T(8,128)} %get-tuple-element.75), calls=%async_computation.3 | async-start | bytes 25165824 | tf_op jit(solution)/shard_map/all_to_all | solution.py:112
  309.1 2.4 copy.278
  315.4 3.2 copy-done.3
  318.6 2.9 fusion.38
  322.9 13.2 %copy.266 = f32[24,256,4,128]{3,0,2,1:T(8,128)} copy(f32[24,256,4,128]{1,3,2,0:T(8,128)} %bitcast.165) | data formatting | bytes 25165824 | tf_op jit(solution)/shard_map/reshape | solution.py:133
  337.6 108.3 %all-to-all-done.3 = f32[8,3,256,4,128]{2,4,3,1,0:T(8,128)} async-done(((f32[8,3,256,4,128]{2,4,3,1,0:T(8,128)}), f32[8,3,256,4,128]{2,4,3,1,0:T(8,128)}, u32[]{:S(2)}, u32[]{:S(2)}) %all-to-all-start.3) | async-done | bytes 12582944 | tf_op jit(solution)/shard_map/all_to_all | solution.py:112
  445.9 12.9 %copy.267 = f32[24,256,4,128]{3,0,2,1:T(8,128)} copy(f32[24,256,4,128]{1,3,2,0:T(8,128)} %bitcast.49) | data formatting | bytes 25165824 | tf_op jit(solution)/shard_map/reshape | solution.py:134
  458.8 15.0 %fusion.33 = f32[8,256,4,128]{3,0,2,1:T(8,128)S(1)} fusion(f32[24,256,4,128]{3,0,2,1:T(8,128)} %copy.267, f32[24,256,4,128]{3,0,2,1:T(8,128)} %copy.266, f32[48,256,4]{0,2,1:T(4,128)S(1)} %copy.269, s32[48]{0:T(128)S(1)} %pad_add_fusion), kind=kOutput, calls=%fused_computation.50 | convolution fusion | flops 616563072 | bytes 29556928 | tf_op jit(solution)/shard_map/kb,kshd->bshd/dot_general | solution.py:151
  473.9 9.4 %fusion.44 = bf16[8,256,4,128]{3,1,2,0:T(8,128)(2,1)S(1)} fusion(f32[8,256,4,128]{3,0,2,1:T(8,128)S(1)} %fusion.33, f32[8,256,4]{1,2,0:T(4,128)S(1)} %copy.273, f32[8,256,4]{1,2,0:T(4,128)S(1)} %copy.265, f32[8,4,256,256]{2,3,1,0:T(8,128)} %copy-done.3, f32[8,4,256]{2,1,0:T(4,128)S(1)} %get-tuple-element.221, f32[8,4,256]{2,1,0:T(4,128)S(1)} %copy.246, ...), kind=kOutput, calls=%fused_computation.63 | convolution fusion | flops 549453824 | bytes 16973824 | tf_op jit(solution)/shard_map/vmap(hst,thd->shd)/dot_general | solution.py:69
  487.1 53.3 %all_to_all.47 = bf16[4,512,512]{2,1,0:T(8,128)(2,1)S(1)} all-to-all(bf16[4,512,512]{2,1,0:T(8,128)(2,1)} %convert_element_type.32), channel_id=1, replica_groups=mesh['seq'=8,'head'=4] {'head'}, dimensions={0} | all-to-all | bytes 4194304 | tf_op jit(solution)/shard_map/all_to_all | solution.py:159
  540.4 2.4 copy.275
  542.8 9.9 %convolution_convert_fusion = bf16[512,2048]{1,0:T(8,128)(2,1)} fusion(bf16[512,2048]{0,1:T(8,128)(2,1)} %bitcast.168, bf16[2048,2048]{1,0:T(8,128)(2,1)} %all-gather.2.cloned.1.call-done), kind=kOutput, calls=%fused_computation.69 | convolution fusion | flops 4296015872 | bytes 12582912 | tf_op jit(solution)/shard_map/dot_general | solution.py:160
  (130 shorter events, 47.0 us)
Async XLA Ops:
  6.5 49.5 %copy-start = (s32[64,16]{0,1:T(8,128)S(1)}, s32[64,16]{0,1:T(8,128)}, u32[]{:S(2)}) copy-start(s32[64,16]{0,1:T(8,128)} %param.11) | copy-start | bytes 12292
  7.9 11.3 %all-to-all-start = ((s32[1,8,3]{2,0,1:T(1,128)}), s32[1,8,3]{2,0,1:T(1,128)S(1)}, u32[]{:S(2)}, u32[]{:S(2)}) async-start(s32[1,8,3]{2,0,1:T(1,128)} %copy.252), calls=%async_computation | async-start | bytes 8192 | tf_op jit(solution)/shard_map/all_to_all | solution.py:87
  32.3 148.1 %all-to-all-start.1 = ((bf16[8,3,256,4,128]{2,4,3,1,0:T(8,128)(2,1)}), bf16[8,3,256,4,128]{2,4,3,1,0:T(8,128)(2,1)}, u32[]{:S(2)}, u32[]{:S(2)}) async-start(bf16[8,3,256,4,128]{2,4,3,1,0:T(8,128)(2,1)} %copy.261), calls=%async_computation.1 | async-start | bytes 12582912 | tf_op jit(solution)/shard_map/all_to_all | solution.py:94
  37.1 7.5 %copy-start.5 = (s32[1,8,3]{1,0,2:T(1,128)S(1)}, s32[1,8,3]{1,0,2:T(1,128)}, u32[]{:S(2)}) copy-start(s32[1,8,3]{1,0,2:T(1,128)} %param.12) | copy-start | bytes 292
  55.8 67.0 %collective-permute-start = (bf16[1,3,256,4,128]{4,2,3,1,0:T(8,128)(2,1)}, bf16[1,3,256,4,128]{4,2,3,1,0:T(8,128)(2,1)}, u32[]{:S(2)}, u32[]{:S(2)}) collective-permute-start(bf16[1,3,256,4,128]{4,2,3,1,0:T(8,128)(2,1)} %get-tuple-element.215), channel_id=1, source_target_pairs={{0,4},{4,8},{8,12},{12,16},{16,20},{20,24},{24,28},{28,0},{1,5},{5... | collective-permute-start | bytes 2359304 | tf_op jit(solution)/shard_map/ppermute | solution.py:29
  62.1 6.6 %copy-start.6 = (s32[1,8]{1,0:T(1,128)S(1)}, s32[1,8]{1,0:T(1,128)}, u32[]{:S(2)}) copy-start(s32[1,8]{1,0:T(1,128)} %param.14) | copy-start | bytes 100
  67.2 60.0 %collective-permute-start.1 = (bf16[1,3,256,4,128]{4,2,3,1,0:T(8,128)(2,1)}, bf16[1,3,256,4,128]{4,2,3,1,0:T(8,128)(2,1)}, u32[]{:S(2)}, u32[]{:S(2)}) collective-permute-start(bf16[1,3,256,4,128]{4,2,3,1,0:T(8,128)(2,1)} %get-tuple-element.214), channel_id=1, source_target_pairs={{0,8},{4,12},{8,16},{12,20},{16,24},{20,28},{24,0},{28,4},{1,9},{5... | collective-permute-start | bytes 2359304 | tf_op jit(solution)/shard_map/ppermute | solution.py:29
  68.8 74.7 %collective-permute-start.2 = (bf16[1,3,256,4,128]{4,2,3,1,0:T(8,128)(2,1)}, bf16[1,3,256,4,128]{4,2,3,1,0:T(8,128)(2,1)}, u32[]{:S(2)}, u32[]{:S(2)}) collective-permute-start(bf16[1,3,256,4,128]{4,2,3,1,0:T(8,128)(2,1)} %get-tuple-element.213), channel_id=1, source_target_pairs={{0,12},{4,16},{8,20},{12,24},{16,28},{20,0},{24,4},{28,8},{1,13},{... | collective-permute-start | bytes 2359304 | tf_op jit(solution)/shard_map/ppermute | solution.py:29
  69.9 75.7 %collective-permute-start.3 = (bf16[1,3,256,4,128]{4,2,3,1,0:T(8,128)(2,1)}, bf16[1,3,256,4,128]{4,2,3,1,0:T(8,128)(2,1)S(1)}, u32[]{:S(2)}, u32[]{:S(2)}) collective-permute-start(bf16[1,3,256,4,128]{4,2,3,1,0:T(8,128)(2,1)} %get-tuple-element.212), channel_id=1, source_target_pairs={{0,16},{4,20},{8,24},{12,28},{16,0},{20,4},{24,8},{28,12},{1,17},{... | collective-permute-start | bytes 2359304 | tf_op jit(solution)/shard_map/ppermute | solution.py:29
  71.5 85.7 %collective-permute-start.4 = (bf16[1,3,256,4,128]{4,2,3,1,0:T(8,128)(2,1)}, bf16[1,3,256,4,128]{4,2,3,1,0:T(8,128)(2,1)S(1)}, u32[]{:S(2)}, u32[]{:S(2)}) collective-permute-start(bf16[1,3,256,4,128]{4,2,3,1,0:T(8,128)(2,1)} %get-tuple-element.211), channel_id=1, source_target_pairs={{0,20},{4,24},{8,28},{12,0},{16,4},{20,8},{24,12},{28,16},{1,21},{... | collective-permute-start | bytes 2359304 | tf_op jit(solution)/shard_map/ppermute | solution.py:29
  122.8 35.5 %collective-permute-start.5 = (bf16[1,3,256,4,128]{4,2,3,1,0:T(8,128)(2,1)}, bf16[1,3,256,4,128]{4,2,3,1,0:T(8,128)(2,1)S(1)}, u32[]{:S(2)}, u32[]{:S(2)}) collective-permute-start(bf16[1,3,256,4,128]{4,2,3,1,0:T(8,128)(2,1)} %get-tuple-element.210), channel_id=1, source_target_pairs={{0,24},{4,28},{8,0},{12,4},{16,8},{20,12},{24,16},{28,20},{1,25},{... | collective-permute-start | bytes 2359304 | tf_op jit(solution)/shard_map/ppermute | solution.py:29
  127.2 45.5 %collective-permute-start.6 = (bf16[1,3,256,4,128]{4,2,3,1,0:T(8,128)(2,1)S(1)}, bf16[1,3,256,4,128]{4,2,3,1,0:T(8,128)(2,1)S(1)}, u32[]{:S(2)}, u32[]{:S(2)}) collective-permute-start(bf16[1,3,256,4,128]{4,2,3,1,0:T(8,128)(2,1)S(1)} %get-tuple-element.209), channel_id=1, source_target_pairs={{0,28},{4,0},{8,4},{12,8},{16,12},{20,16},{24,20},{28,24},{1,29},{... | collective-permute-start | bytes 2359304 | tf_op jit(solution)/shard_map/ppermute | solution.py:29
  301.2 7.9 %copy-start.2 = (bf16[8,256,4,128]{3,2,1,0:T(4,128)(2,1)S(1)}, bf16[8,256,4,128]{3,2,1,0:T(4,128)(2,1)}, u32[]{:S(2)}) copy-start(bf16[8,256,4,128]{3,2,1,0:T(4,128)(2,1)} %reshape.382) | copy-start | bytes 6291460
  301.2 144.7 %all-to-all-start.3 = ((f32[8,3,256,4,128]{2,4,3,1,0:T(8,128)}), f32[8,3,256,4,128]{2,4,3,1,0:T(8,128)}, u32[]{:S(2)}, u32[]{:S(2)}) async-start(f32[8,3,256,4,128]{2,4,3,1,0:T(8,128)} %get-tuple-element.75), calls=%async_computation.3 | async-start | bytes 25165824 | tf_op jit(solution)/shard_map/all_to_all | solution.py:112
  308.3 234.5 %all-gather.2.cloned.1.call-start = ((), (), s32[]{:S(2)}) async-start(), calls=%async_computation.6 | async-start | bytes 10485760 | tf_op jit(solution)/shard_map/all_gather | solution.py:161
  315.4 3.2 copy-start.3
  458.8 15.0 %copy-start.4 = (bf16[8,256,4,128]{3,2,1,0:T(4,128)(2,1)S(1)}, bf16[8,256,4,128]{3,2,1,0:T(4,128)(2,1)}, u32[]{:S(2)}) copy-start(bf16[8,256,4,128]{3,2,1,0:T(4,128)(2,1)} %reshape.383) | copy-start | bytes 6291460
  542.8 9.9 %copy-start.1 = (s32[64,16]{0,1:T(8,128)S(1)}, s32[64,16]{0,1:T(8,128)}, u32[]{:S(2)}) copy-start(s32[64,16]{0,1:T(8,128)} %param.11) | copy-start | bytes 12292
Sparse Core Ops, SparseCore 0:
  310.7 150.7 all-gather.1
